TPU v7x, 32 devices: a whole 2x2x4 slice. The times are simulated.
32 devices in a mesh: groups: 2 (over y), ctx: 16 (over z, x, core).
Axes of the slice: x: 2, y: 2, z: 4, core: 2. Of those that a mesh axis runs over, the one named last changes fastest.
Arguments:
- queries: bfloat16 [512, 5120], P(('groups', 'ctx')), parts along dimension 0, may hold values from -45 to 45
- keys: bfloat16 [49152, 1024], P(('groups', 'ctx')), parts along dimension 0, may hold values from -5 to 5
- values: bfloat16 [49152, 1024], P(('groups', 'ctx')), parts along dimension 0, may hold values from -10 to 10
- block_mask: int32 [16, 2, 192], P('groups', None, 'ctx'), parts along dimension 0, may hold values from 0 to 1, as said below
- out_weight: bfloat16 [5120, 5120], P('ctx'), may hold values from -0.078125 to 0.078125
Outputs:
- projected: bfloat16 [512, 5120], P(('groups', 'ctx')), parts along dimension 0
There are 2 independent parts, one for each index of `groups`. A program takes and returns all parts, laid end to end along the dimension named above; an argument that names none is the same for every part. Nothing has to cross between parts.
Inputs may be any that keep to these rules, and one draw needn't show every extreme that they name: `block_mask`: for every key head and query block at least one key block is 1; the share of 1s differs between spans of 1536 positions.
All inputs are finite; a program needn't handle non-finite values.
Results may differ from a plain program's by a relative error of at most 0.0055.
Values may be sent and summed in bfloat16 or wider, within the bound.
A program may use at most 128 MiB of HBM per device.

v0:
```python
import math
import jax
import jax.numpy as jnp
from jax import lax
from jax.sharding import PartitionSpec as P

HEAD_SIZE = 128
NEG = -1e30


def shards(queries, keys, values, block_mask, out_weight):
    whole = lax.all_gather(queries, "ctx", axis=0, tiled=True)
    qtok, width = whole.shape
    kdev = keys.shape[0]
    heads_kv, query_block_count, key_block_count = block_mask.shape
    head_dim = HEAD_SIZE
    query_group = width // head_dim // heads_kv
    scale = 1.0 / math.sqrt(head_dim)
    query_tensor = whole.reshape(qtok, heads_kv, query_group, head_dim)
    key_tensor = keys.reshape(kdev, heads_kv, head_dim)
    value_tensor = values.reshape(kdev, heads_kv, head_dim)

    def head_scores(head):
        q_h = lax.dynamic_index_in_dim(query_tensor, head, 1, keepdims=False)
        k_h = lax.dynamic_index_in_dim(key_tensor, head, 1, keepdims=False)
        scores = jnp.einsum("qge,ke->gqk", q_h, k_h, preferred_element_type=jnp.float32) * scale
        blocks = lax.dynamic_index_in_dim(block_mask, head, 0, keepdims=False)
        live = jnp.broadcast_to(
            blocks[:, None, :, None] > 0,
            (
                query_block_count,
                qtok // query_block_count,
                key_block_count,
                kdev // key_block_count,
            ),
        )
        return (scores, live.reshape(qtok, kdev))

    def max_step(head, maxima):
        scores, live = head_scores(head)
        local = jnp.max(jnp.where(live[None], scores, NEG), axis=2)
        return lax.dynamic_update_slice(maxima, local.T[:, None, :], (0, head, 0))

    maxima = lax.fori_loop(
        0, heads_kv, max_step, jnp.full((qtok, heads_kv, query_group), NEG, jnp.float32)
    )
    row_max = lax.pmax(maxima, "ctx")

    def sum_step(head, carry):
        numer, denom = carry
        scores, live = head_scores(head)
        top = lax.dynamic_index_in_dim(row_max, head, 1, keepdims=False).T[:, :, None]
        probs = jnp.where(live[None], jnp.exp(scores - top), 0.0).astype(jnp.bfloat16)
        total = jnp.sum(probs.astype(jnp.float32), axis=2)
        v_h = lax.dynamic_index_in_dim(value_tensor, head, 1, keepdims=False)
        weighted = jnp.einsum("gqk,ke->qge", probs, v_h, preferred_element_type=jnp.float32)
        numer = lax.dynamic_update_slice(
            numer, weighted.reshape(qtok, 1, query_group * head_dim), (0, head, 0)
        )
        denom = lax.dynamic_update_slice(denom, total.T[:, None, :], (0, head, 0))
        return (numer, denom)

    start_numer = jnp.zeros((qtok, heads_kv, query_group * head_dim), jnp.float32)
    start_denom = jnp.zeros((qtok, heads_kv, query_group), jnp.float32)
    numer, denom = lax.fori_loop(0, heads_kv, sum_step, (start_numer, start_denom))
    numer = numer.reshape(qtok, width)
    denom = denom.reshape(qtok, heads_kv * query_group)
    num_rows, den_rows = (
        lax.psum_scatter(numer, "ctx", scatter_dimension=0, tiled=True),
        lax.psum_scatter(denom, "ctx", scatter_dimension=0, tiled=True),
    )
    own_rows = num_rows.shape[0]
    attn_rows = (num_rows.reshape(own_rows, -1, head_dim) / den_rows[:, :, None]).reshape(
        own_rows, width
    )
    attn_cols = lax.all_to_all(
        attn_rows.astype(jnp.bfloat16), "ctx", split_axis=1, concat_axis=0, tiled=True
    )
    summed = lax.psum_scatter(
        jnp.dot(attn_cols, out_weight, preferred_element_type=jnp.float32),
        "ctx",
        scatter_dimension=0,
        tiled=True,
    )
    return summed.astype(jnp.bfloat16)


def solution(mesh):
    return jax.shard_map(
        shards,
        mesh=mesh,
        in_specs=(
            P(("groups", "ctx"), None),
            P(("groups", "ctx"), None),
            P(("groups", "ctx"), None),
            P("groups", None, "ctx"),
            P("ctx", None),
        ),
        out_specs=P(("groups", "ctx"), None),
        check_vma=False,
    )
```

profile of v0, /device:TPU:0, one launch (start us, length us, event | category | flops | bytes accessed | tf_op | source)
XLA Modules:
  0.0 496.8 jit_solution(2088119072019379952)
XLA Ops:
  7.3 4.9 copy.38
  12.2 4.7 copy.42
  16.9 4.7 copy.37
  21.6 34.0 %all-gather.2.cloned.1.call-done = bf16[256,5120]{1,0:T(8,128)(2,1)} async-done(((bf16[16,5120]{1,0:T(8,128)(2,1)}), bf16[256,5120]{1,0:T(8,128)(2,1)}) %all-gather.2.cloned.1.call-update) | async-done | bytes 2621456 | tf_op jit(solution)/shard_map/all_gather | solution.py:12
  55.6 4.4 copy.39
  60.0 4.3 copy.43
  64.3 53.1 %while.28 = (s32[]{:T(128)}, f32[256,8,5]{0,2,1:T(8,128)S(1)}, s32[8,2,12]{2,1,0:T(2,128)}, bf16[1536,8,128]{2,0,1:T(8,128)(2,1)}, bf16[256,8,5,128]{3,0,2,1:T(8,128)(2,1)}, /*index=5*/s32[]{:T(128)}) while((s32[]{:T(128)}, f32[256,8,5]{0,2,1:T(8,128)S(1)}, s32[8,2,12]{2,1,0:T(2,128)}, bf16[1536,8,128]{2,0,1:T(8,128)(2,1)}, ...), condition=%wide.region_2.3_spmd, body=%wide.region_0.2_spmd.sunk | while | flops 509213472 | bytes 3102949 | solution.py:44
  66.1 2.2 copy.63
  68.4 2.5 fusion.31
  72.8 2.2 copy.63
  75.0 2.5 fusion.31
  79.4 2.2 copy.63
  81.6 2.5 fusion.31
  86.1 2.2 copy.63
  88.3 2.5 fusion.31
  92.7 2.2 copy.63
  94.9 2.5 fusion.31
  99.3 2.2 copy.63
  101.5 2.5 fusion.31
  106.0 2.2 copy.63
  108.2 2.5 fusion.31
  112.6 2.2 copy.63
  114.8 2.5 fusion.31
  117.4 59.4 %pmax.7 = f32[256,8,5]{0,2,1:T(8,128)S(1)} all-reduce(f32[256,8,5]{0,2,1:T(8,128)S(1)} %get-tuple-element.239), channel_id=1, replica_groups=mesh['groups'=2,'ctx'=16] {'ctx'}, use_global_device_ids=true, to_apply=%region_3.4 | all-reduce | flops 10240 | bytes 81920 | tf_op jit(solution)/shard_map/pmax | solution.py:47
  176.8 80.6 %while.29 = (s32[]{:T(128)}, f32[256,8,640]{0,2,1:T(8,128)}, f32[256,8,5]{0,2,1:T(8,128)S(1)}, bf16[1536,8,128]{0,2,1:T(8,128)(2,1)}, s32[8,2,12]{2,1,0:T(2,128)...) while((s32[]{:T(128)}, f32[256,8,640]{0,2,1:T(8,128)}, ...), condition=%wide.region_6.7_spmd, body=%wide.region_4.6_spmd.sunk | while | flops 1018428160 | bytes 13341961 | solution.py:65
  178.7 2.2 copy.65
  180.9 3.4 convert_reduce_fusion.2
  188.7 2.2 copy.65
  190.9 3.4 convert_reduce_fusion.2
  198.8 2.2 copy.65
  201.0 3.4 convert_reduce_fusion.2
  208.9 2.2 copy.65
  211.1 3.4 convert_reduce_fusion.2
  219.0 2.2 copy.65
  221.2 3.4 convert_reduce_fusion.2
  229.1 2.2 copy.65
  231.3 3.4 convert_reduce_fusion.2
  239.1 2.2 copy.65
  241.3 3.4 convert_reduce_fusion.2
  249.2 2.2 copy.65
  251.4 3.4 convert_reduce_fusion.2
  258.3 6.0 %copy.44 = f32[256,5120]{1,0:T(8,128)} copy(f32[256,5120]{0,1:T(8,128)} %bitcast.123) | data formatting | bytes 10485760 | tf_op jit(solution)/shard_map/reshape | solution.py:66
  264.3 46.3 %reduce-scatter.10.cloned.1.call-done = f32[16,40]{1,0:T(8,128)} async-done(((f32[256,40]{1,0:T(8,128)}), f32[16,40]{1,0:T(8,128)}) %reduce-scatter.10.cloned.1.call-update) | async-done | bytes 2576 | tf_op jit(solution)/shard_map/reduce_scatter | solution.py:70
  310.7 81.4 %reduce-scatter.6.cloned.1.call-done = f32[16,5120]{1,0:T(8,128)} async-done(((f32[256,5120]{1,0:T(8,128)}), f32[16,5120]{1,0:T(8,128)}) %reduce-scatter.6.cloned.1.call-update) | async-done | bytes 327696 | tf_op jit(solution)/shard_map/reduce_scatter | solution.py:69
  392.9 1.7 fusion.18
  395.7 12.4 %all_to_all.19 = bf16[16,16,320]{2,0,1:T(8,128)(2,1)S(1)} all-to-all(bf16[16,16,320]{2,0,1:T(8,128)(2,1)S(1)} %copy.46), channel_id=1, replica_groups=mesh['groups'=2,'ctx'=16] {'ctx'}, dimensions={1} | all-to-all | bytes 327680 | tf_op jit(solution)/shard_map/all_to_all | solution.py:76
  408.2 3.9 fusion.19
  412.1 76.6 %reduce-scatter.8.cloned.1.call-done = f32[16,5120]{1,0:T(8,128)} async-done(((f32[256,5120]{1,0:T(8,128)}), f32[16,5120]{1,0:T(8,128)}) %reduce-scatter.8.cloned.1.call-update) | async-done | bytes 327696 | tf_op jit(solution)/shard_map/reduce_scatter | solution.py:79
  (107 shorter events, 55.4 us)
Async XLA Ops:
  6.5 401.6 %copy-start = (bf16[320,5120]{1,0:T(8,128)(2,1)S(1)}, bf16[320,5120]{1,0:T(8,128)(2,1)}, u32[]{:S(2)}) copy-start(bf16[320,5120]{1,0:T(8,128)(2,1)} %param.13) | copy-start | bytes 9830404
  6.5 49.0 %all-gather.2.cloned.1.call-start = ((), (), s32[]{:S(2)}) async-start(), calls=%async_computation.4 | async-start | bytes 2785280 | tf_op jit(solution)/shard_map/all_gather | solution.py:12
  7.3 303.4 %reduce-scatter.10.cloned.1.call-start = ((), (), s32[]{:S(2)}) async-start(), calls=%async_computation.7 | async-start | bytes 139264 | tf_op jit(solution)/shard_map/reduce_scatter | solution.py:70
  258.2 133.8 %reduce-scatter.6.cloned.1.call-start = ((), (), s32[]{:S(2)}) async-start(), calls=%async_computation.5 | async-start | bytes 5570560 | tf_op jit(solution)/shard_map/reduce_scatter | solution.py:69
  264.3 224.4 %reduce-scatter.8.cloned.1.call-start = ((), (), s32[]{:S(2)}) async-start(), calls=%async_computation.6 | async-start | bytes 5570560 | tf_op jit(solution)/shard_map/reduce_scatter | solution.py:79
Sparse Core Ops, SparseCore 0:
  9.6 45.8 all-gather.1
  258.4 52.2 reduce-scatter.9
  314.5 77.4 reduce-scatter.5
  412.2 76.4 reduce-scatter.7
where the time goes:
time: 499 us; the launch traced here: 497 us
  waiting for transfers between devices  239 us (48%)
  local copies, waits for them, and re-layouts  92.9 us (19%)
  blocking collectives  71.9 us (14%)
  matrix products  64.9 us (13%)
  other arithmetic  14.3 us (3%)
  between operations  13.2 us (3%)
    reduce_scatter x1, waiting for transfers between devices, shards(): lax.psum_scatter(numer, 'ctx', scatter_dimension=0, tiled=True)  81.4 us
    reduce_scatter x1, waiting for transfers between devices, shards(): lax.psum_scatter(jnp.dot(attn_cols, out_weight, preferred_element_type=jn...  76.6 us
    pmax x1, blocking collectives, shards(): row_max = lax.pmax(maxima, 'ctx')  59.4 us
    dot_general x16, matrix products, head_scores(): jnp.einsum('qge,ke->gqk', q_h, k_h, preferred_element_type=jnp.float32)  47.6 us
    reduce_scatter x1, waiting for transfers between devices, shards(): lax.psum_scatter(denom, 'ctx', scatter_dimension=0, tiled=True)  46.3 us
    all_gather x1, waiting for transfers between devices, shards(): whole = lax.all_gather(queries, 'ctx', axis=0, tiled=True)  34 us
    broadcast_in_dim x8, local copies, waits for them, and re-layouts, max_step(): local = jnp.max(jnp.where(live[None], scores, NEG), axis=2)  17.8 us
    broadcast_in_dim x8, local copies, waits for them, and re-layouts, sum_step(): jnp.where(live[None], jnp.exp(scores - top), 0.0).astype(jnp.bfloat16)  17.8 us
  transfers between devices with their start and end apart: 4, of which 4 were waited for; matrix products, arithmetic and copies ran while one was open for 4% of the time, Pallas kernels for 0%

commit v1 on v0

--- a/solution.py
+++ b/solution.py
@@ -8,8 +8,20 @@
 NEG = -1e30
 
 
+def doubled_up(x, axis, dim):
+    ways, here = (lax.axis_size(axis), lax.axis_index(axis))
+    grown, reach = (x, 1)
+    while reach < ways:
+        theirs = lax.ppermute(grown, axis, [(d, d ^ reach) for d in range(ways)])
+        mine_first = jnp.concatenate([grown, theirs], axis=dim)
+        theirs_first = jnp.concatenate([theirs, grown], axis=dim)
+        grown = jnp.where(here & reach == 0, mine_first, theirs_first)
+        reach = 2 * reach
+    return grown
+
+
 def shards(queries, keys, values, block_mask, out_weight):
-    whole = lax.all_gather(queries, "ctx", axis=0, tiled=True)
+    whole = doubled_up(queries, "ctx", 0)
     qtok, width = whole.shape
     kdev = keys.shape[0]
     heads_kv, query_block_count, key_block_count = block_mask.shape

time: 499 us -> 572 us (1.15)
  other arithmetic: 14.3 us -> 43.4 us
  local copies, waits for them, and re-layouts: 92.9 us -> 113 us
  waiting for transfers between devices: 239 us -> 253 us
  starting transfers between devices: 0.12 us -> 7.74 us
    ppermute x0 -> x4, waiting for transfers between devices: none -> 49.1 us  [doubled_up(): theirs = lax.ppermute(grown, axis, [(d, d ^ reach) for d in range(ways)])]
    all_gather x1 -> x0, waiting for transfers between devices: 34 us -> none  [shards(): whole = lax.all_gather(queries, 'ctx', axis=0, tiled=True)]
    select_n x0 -> x7, other arithmetic: none -> 27 us  [doubled_up(): grown = jnp.where(here & reach == 0, mine_first, theirs_first)]
    concatenate x0 -> x7, local copies, waits for them, and re-layouts: none -> 16.1 us  [the longest x6 13.8 us: doubled_up(): mine_first = jnp.concatenate([grown, theirs], axis=dim)]
    ppermute x0 -> x4, starting transfers between devices: none -> 7.66 us  [doubled_up(): theirs = lax.ppermute(grown, axis, [(d, d ^ reach) for d in range(ways)])]
  transfers between devices with their start and end apart: 4 -> 7, of which waited for: 4 -> 7; matrix products, arithmetic and copies ran while one was open for 4% -> 7% of each run, Pallas kernels for 0% -> 0%
where the time goes in v1:
time: 572 us; the launch traced here: 570 us
  waiting for transfers between devices  253 us (44%)
  local copies, waits for them, and re-layouts  113 us (20%)
  blocking collectives  73.7 us (13%)
  matrix products  64.9 us (11%)
  other arithmetic  43.4 us (8%)
  between operations  13.2 us (2%)
  starting transfers between devices  7.74 us (1%)
    reduce_scatter x1, waiting for transfers between devices, shards(): lax.psum_scatter(numer, 'ctx', scatter_dimension=0, tiled=True)  81.3 us
    reduce_scatter x1, waiting for transfers between devices, shards(): lax.psum_scatter(jnp.dot(attn_cols, out_weight, preferred_element_type=jn...  76.5 us
    pmax x1, blocking collectives, shards(): row_max = lax.pmax(maxima, 'ctx')  61.2 us
    ppermute x4, waiting for transfers between devices, doubled_up(): theirs = lax.ppermute(grown, axis, [(d, d ^ reach) for d in range(ways)])  49.1 us
    dot_general x16, matrix products, head_scores(): jnp.einsum('qge,ke->gqk', q_h, k_h, preferred_element_type=jnp.float32)  47.6 us
    reduce_scatter x1, waiting for transfers between devices, shards(): lax.psum_scatter(denom, 'ctx', scatter_dimension=0, tiled=True)  46.5 us
    select_n x7, other arithmetic, doubled_up(): grown = jnp.where(here & reach == 0, mine_first, theirs_first)  27 us
    broadcast_in_dim x8, local copies, waits for them, and re-layouts, max_step(): local = jnp.max(jnp.where(live[None], scores, NEG), axis=2)  17.9 us
  transfers between devices with their start and end apart: 7, of which 7 were waited for; matrix products, arithmetic and copies ran while one was open for 7% of the time, Pallas kernels for 0%

profile of v1, /device:TPU:0, one launch (start us, length us, event | category | flops | bytes accessed | tf_op | source)
XLA Modules:
  0.0 569.6 jit_solution(486515067442725495)
XLA Ops:
  10.2 2.3 copy.54
  12.5 2.3 copy.53
  14.7 2.5 broadcast_select_fusion
  19.4 2.9 collective-permute-start.1
  22.3 8.3 %collective-permute-done.1 = bf16[32,5120]{1,0:T(8,128)(2,1)} collective-permute-done((bf16[32,5120]{1,0:T(8,128)(2,1)}, bf16[32,5120]{1,0:T(8,128)(2,1)}, u32[]{:S(2)}, u32[]{:S(2)}) %collective-permute-start.1) | collective-permute-done | bytes 327712 | tf_op jit(solution)/shard_map/ppermute | solution.py:15
  30.6 2.3 copy.56
  32.9 5.0 maximum_select_fusion.2
  37.9 2.3 copy.58
  42.0 14.8 %collective-permute-done.2 = bf16[64,5120]{1,0:T(8,128)(2,1)} collective-permute-done((bf16[64,5120]{1,0:T(8,128)(2,1)}, bf16[64,5120]{1,0:T(8,128)(2,1)}, u32[]{:S(2)}, u32[]{:S(2)}) %collective-permute-start.2) | collective-permute-done | bytes 655392 | tf_op jit(solution)/shard_map/ppermute | solution.py:15
  56.7 2.3 copy.59
  59.0 5.0 maximum_select_fusion.3
  64.0 2.5 collective-permute-start.3
  67.7 4.7 copy.52
  72.4 4.7 copy.65
  77.1 4.7 copy.51
  87.8 2.9 maximum_select_fusion.4
  90.8 2.6 concatenate.65
  93.4 4.6 maximum_select_fusion.1
  98.0 24.7 %collective-permute-done.3 = bf16[128,5120]{0,1:T(8,128)(2,1)} collective-permute-done((bf16[128,5120]{0,1:T(8,128)(2,1)}, bf16[128,5120]{0,1:T(8,128)(2,1)}, u32[]{:S(2)}, u32[]{:S(2)}) %collective-permute-start.3) | collective-permute-done | bytes 1310752 | tf_op jit(solution)/shard_map/ppermute | solution.py:15
  122.8 3.8 copy.61
  126.6 4.9 maximum_select_fusion
  131.5 3.6 copy.66
  135.1 53.2 %while.28 = (s32[]{:T(128)}, f32[256,8,5]{0,2,1:T(8,128)S(1)}, s32[8,2,12]{2,1,0:T(2,128)}, bf16[1536,8,128]{2,0,1:T(8,128)(2,1)}, bf16[256,8,5,128]{3,0,2,1:T(8,128)(2,1)}, /*index=5*/s32[]{:T(128)}) while((s32[]{:T(128)}, f32[256,8,5]{0,2,1:T(8,128)S(1)}, s32[8,2,12]{2,1,0:T(2,128)}, bf16[1536,8,128]{2,0,1:T(8,128)(2,1)}, ...), condition=%wide.region_2.3_spmd, body=%wide.region_0.2_spmd.sunk | while | flops 509213472 | bytes 3102949 | solution.py:56
  139.2 2.5 fusion.31
  145.9 2.5 fusion.31
  150.3 2.2 copy.86
  152.5 2.5 fusion.31
  159.2 2.5 fusion.31
  165.8 2.5 fusion.31
  172.5 2.5 fusion.31
  179.1 2.5 fusion.31
  185.8 2.5 fusion.31
  188.3 61.2 %pmax.7 = f32[256,8,5]{0,2,1:T(8,128)S(1)} all-reduce(f32[256,8,5]{0,2,1:T(8,128)S(1)} %get-tuple-element.239), channel_id=1, replica_groups=mesh['groups'=2,'ctx'=16] {'ctx'}, use_global_device_ids=true, to_apply=%region_3.4 | all-reduce | flops 10240 | bytes 81920 | tf_op jit(solution)/shard_map/pmax | solution.py:59
  249.6 80.7 %while.29 = (s32[]{:T(128)}, f32[256,8,640]{0,2,1:T(8,128)}, f32[256,8,5]{0,2,1:T(8,128)S(1)}, bf16[1536,8,128]{0,2,1:T(8,128)(2,1)}, s32[8,2,12]{2,1,0:T(2,128)...) while((s32[]{:T(128)}, f32[256,8,640]{0,2,1:T(8,128)}, ...), condition=%wide.region_6.7_spmd, body=%wide.region_4.6_spmd.sunk | while | flops 1018428160 | bytes 13341961 | solution.py:77
  253.6 3.4 convert_reduce_fusion.2
  263.7 3.4 convert_reduce_fusion.2
  273.8 3.4 convert_reduce_fusion.2
  283.9 3.4 convert_reduce_fusion.2
  294.0 3.4 convert_reduce_fusion.2
  304.1 3.4 convert_reduce_fusion.2
  314.2 3.4 convert_reduce_fusion.2
  324.3 3.4 convert_reduce_fusion.2
  331.1 5.9 %copy.67 = f32[256,5120]{1,0:T(8,128)} copy(f32[256,5120]{0,1:T(8,128)} %bitcast.122) | data formatting | bytes 10485760 | tf_op jit(solution)/shard_map/reshape | solution.py:78
  337.1 46.5 %reduce-scatter.10.cloned.1.call-done = f32[16,40]{1,0:T(8,128)} async-done(((f32[256,40]{1,0:T(8,128)}), f32[16,40]{1,0:T(8,128)}) %reduce-scatter.10.cloned.1.call-update) | async-done | bytes 2576 | tf_op jit(solution)/shard_map/reduce_scatter | solution.py:82
  383.6 81.3 %reduce-scatter.6.cloned.1.call-done = f32[16,5120]{1,0:T(8,128)} async-done(((f32[256,5120]{1,0:T(8,128)}), f32[16,5120]{1,0:T(8,128)}) %reduce-scatter.6.cloned.1.call-update) | async-done | bytes 327696 | tf_op jit(solution)/shard_map/reduce_scatter | solution.py:81
  468.6 12.5 %all_to_all.19 = bf16[16,16,320]{2,0,1:T(8,128)(2,1)S(1)} all-to-all(bf16[16,16,320]{2,0,1:T(8,128)(2,1)S(1)} %copy.69), channel_id=1, replica_groups=mesh['groups'=2,'ctx'=16] {'ctx'}, dimensions={1} | all-to-all | bytes 327680 | tf_op jit(solution)/shard_map/all_to_all | solution.py:88
  481.1 3.9 fusion.19
  484.9 76.5 %reduce-scatter.8.cloned.1.call-done = f32[16,5120]{1,0:T(8,128)} async-done(((f32[256,5120]{1,0:T(8,128)}), f32[16,5120]{1,0:T(8,128)}) %reduce-scatter.8.cloned.1.call-update) | async-done | bytes 327696 | tf_op jit(solution)/shard_map/reduce_scatter | solution.py:91
  (136 shorter events, 104.7 us)
Async XLA Ops:
  6.5 474.5 %copy-start = (bf16[320,5120]{1,0:T(8,128)(2,1)S(1)}, bf16[320,5120]{1,0:T(8,128)(2,1)}, u32[]{:S(2)}) copy-start(bf16[320,5120]{1,0:T(8,128)(2,1)} %param.13) | copy-start | bytes 9830404
  6.5 377.0 %reduce-scatter.10.cloned.1.call-start = ((), (), s32[]{:S(2)}) async-start(), calls=%async_computation.6 | async-start | bytes 139264 | tf_op jit(solution)/shard_map/reduce_scatter | solution.py:82
  6.5 1.7 collective-permute-start
  8.2 9.0 %copy-start.1 = (bf16[16,5120]{1,0:T(8,128)(2,1)}, bf16[16,5120]{1,0:T(8,128)(2,1)S(1)}, u32[]{:S(2)}) copy-start(bf16[16,5120]{1,0:T(8,128)(2,1)S(1)} %collective-permute-done) | copy-start | bytes 491524
  19.4 11.2 %collective-permute-start.1 = (bf16[32,5120]{1,0:T(8,128)(2,1)}, bf16[32,5120]{1,0:T(8,128)(2,1)}, u32[]{:S(2)}, u32[]{:S(2)}) collective-permute-start(bf16[32,5120]{1,0:T(8,128)(2,1)} %copy.55), channel_id=1, source_target_pairs={{0,2},{1,3},{2,0},{3,1},{4,6},{5,7},{6,4},{7,5},{8,10},{9,11},{10,... | collective-permute-start | bytes 983048 | tf_op jit(solution)/shard_map/ppermute | solution.py:15
  40.1 16.6 %collective-permute-start.2 = (bf16[64,5120]{1,0:T(8,128)(2,1)}, bf16[64,5120]{1,0:T(8,128)(2,1)}, u32[]{:S(2)}, u32[]{:S(2)}) collective-permute-start(bf16[64,5120]{1,0:T(8,128)(2,1)} %copy.58), channel_id=1, source_target_pairs={{0,4},{1,5},{2,6},{3,7},{4,0},{5,1},{6,2},{7,3},{8,12},{9,13},{10,... | collective-permute-start | bytes 1966088 | tf_op jit(solution)/shard_map/ppermute | solution.py:15
  64.0 58.7 %collective-permute-start.3 = (bf16[128,5120]{0,1:T(8,128)(2,1)}, bf16[128,5120]{0,1:T(8,128)(2,1)}, u32[]{:S(2)}, u32[]{:S(2)}) collective-permute-start(bf16[128,5120]{0,1:T(8,128)(2,1)} %maximum_select_fusion.3), channel_id=1, source_target_pairs={{0,8},{1,9},{2,10},{3,11},{4,12},{5,13},{6,14},{7,15},{8,0},{9,1},... | collective-permute-start | bytes 3932168 | tf_op jit(solution)/shard_map/ppermute | solution.py:15
  131.5 3.6 copy-start.2
  135.1 114.5 %copy-start.3 = (f32[256,8,5]{0,2,1:T(8,128)S(1)}, f32[256,8,5]{0,2,1:T(8,128)}, u32[]{:S(2)}) copy-start(f32[256,8,5]{0,2,1:T(8,128)} %custom-call.2) | copy-start | bytes 122884
  331.1 133.8 %reduce-scatter.6.cloned.1.call-start = ((), (), s32[]{:S(2)}) async-start(), calls=%async_computation.4 | async-start | bytes 5570560 | tf_op jit(solution)/shard_map/reduce_scatter | solution.py:81
  337.1 224.3 %reduce-scatter.8.cloned.1.call-start = ((), (), s32[]{:S(2)}) async-start(), calls=%async_computation.5 | async-start | bytes 5570560 | tf_op jit(solution)/shard_map/reduce_scatter | solution.py:91
Sparse Core Ops, SparseCore 0:
  331.2 52.3 reduce-scatter.9
  387.4 77.3 reduce-scatter.5
  485.1 76.3 reduce-scatter.7
